TPU v7x, 512 devices: a whole 4x4x16 slice. The times are simulated.
512 devices in a mesh: atom: 64 (over y_lo, z, core), kvec: 8 (over y_hi, x).
Axes of the slice: x: 4, y: 4 (y_hi: 2, y_lo: 2; y = y_hi * 2 + y_lo), z: 16, core: 2. Of those that a mesh axis runs over, the one named last changes fastest.
Arguments:
- features: bfloat16 [64, 24576], P(None, 'atom'), may hold values from -6 to 6
- species: int32 [24576], P('atom'), may hold values from 0 to 3
- embed: float32 [4, 64], replicated, may hold values from -4 to 4
- frac_pos: float32 [3, 24576], P(None, 'atom'), may hold values from 0 to 1
- box: float32 [3], replicated, may hold values from 105 to 115
- miller: int32 [3, 8192], P(None, 'kvec'), may hold values from -40 to 40
- filter_weight: float32 [16, 64], replicated, may hold values from -1.5 to 1.5
- cotangent: bfloat16 [64, 24576], P(None, 'atom'), may hold values from -6 to 6
Outputs:
- feat_grad: float32 [64, 24576], P(None, ('atom', 'kvec'))
- force: float32 [3, 24576], P(None, ('atom', 'kvec'))
- filter_grad: float32 [16, 64], replicated
- virial: float32 [3, 3], replicated
All inputs are finite; a program needn't handle non-finite values.
Results may differ from a plain program's by a relative error of at most 0.0051.
Values may be sent and summed in bfloat16 or wider, within the bound.
A program may use at most 64 MiB of HBM per device.

v0:
```python
import math

import jax
import jax.numpy as jnp
from jax import lax
from jax.sharding import PartitionSpec as P

K = 8192
MMAX = 40


TWO_PI = 2.0 * math.pi
PRECISE = lax.Precision.HIGHEST


def radial(q_vals, nbasis):
    q_top = 3.0 * (TWO_PI * MMAX / 105.0) ** 2
    centers = q_top * jnp.arange(nbasis, dtype=jnp.float32) / (nbasis - 1)
    spread_q = 1.5 * q_top / (nbasis - 1)
    offsets = (q_vals[None, :] - centers[:, None]) / spread_q
    radial_basis = jnp.exp(-offsets * offsets)
    radial_slope = -2.0 * offsets / spread_q * radial_basis
    return (radial_basis, radial_slope)


def phases(frac_pos, mill_block):
    m_vals = mill_block.astype(jnp.float32)
    phase_angle = TWO_PI * (
        frac_pos[0][:, None] * m_vals[0][None, :]
        + frac_pos[1][:, None] * m_vals[1][None, :]
        + frac_pos[2][:, None] * m_vals[2][None, :]
    )
    return (jnp.cos(phase_angle).astype(jnp.bfloat16), jnp.sin(phase_angle).astype(jnp.bfloat16))


def kterms(factors, kvec, filter_weight, grad_scale):
    q_vals = kvec[0] * kvec[0] + kvec[1] * kvec[1] + kvec[2] * kvec[2]
    radial_basis, radial_slope = radial(q_vals, filter_weight.shape[0])
    filter_k = jnp.dot(filter_weight.T, radial_basis, precision=PRECISE)
    filter_slope = jnp.dot(filter_weight.T, radial_slope, precision=PRECISE)
    filtered = (filter_k[None] * factors).astype(jnp.bfloat16)
    energy = factors[0] * factors[2] + factors[1] * factors[3]
    filter_grad = (
        lax.dot_general(radial_basis, energy, (((1,), (1,)), ((), ())), precision=PRECISE)
        * grad_scale
    )
    weight_k = jnp.sum(filter_slope * energy, axis=0)
    virial = -2.0 * grad_scale * jnp.dot(kvec * weight_k[None, :], kvec.T, precision=PRECISE)
    return (filtered, filter_grad, virial)


def per_device(features, species, embed, frac_pos, box, miller, filter_weight, cotangent):
    channels, atoms_local = features.shape
    k_local = miller.shape[1]
    atom_total = atoms_local * lax.axis_size("atom")
    norm_atoms = 1.0 / math.sqrt(atom_total)
    grad_scale = math.sqrt(atom_total) / math.sqrt(K)
    species_ids = jnp.arange(embed.shape[0], dtype=jnp.int32)
    onehot = (species[None, :] == species_ids[:, None]).astype(jnp.float32)
    lookup = jnp.dot(embed.T, onehot, precision=PRECISE)
    hidden = (features.astype(jnp.float32) + lookup).astype(jnp.bfloat16)
    stacked = jnp.concatenate([hidden, cotangent], axis=0)
    kvec = TWO_PI * miller.astype(jnp.float32) / box[:, None]
    block_len = min(512, k_local)
    block_count = k_local // block_len

    def first_pass(block_id, totals):
        offset = (block_id * block_len).astype(jnp.int32)
        mill_block = lax.dynamic_slice_in_dim(miller, offset, block_len, 1)
        cos_tile, sin_tile = phases(frac_pos, mill_block)
        cos_part = jnp.dot(stacked, cos_tile, preferred_element_type=jnp.float32)
        sin_part = jnp.dot(stacked, sin_tile, preferred_element_type=jnp.float32)
        factor_block = (
            jnp.stack(
                [cos_part[:channels], sin_part[:channels], cos_part[channels:], sin_part[channels:]]
            )
            * norm_atoms
        )
        return lax.dynamic_update_slice_in_dim(totals, factor_block, offset, 2)

    partial_value = lax.fori_loop(
        0, block_count, first_pass, jnp.zeros((4, channels, k_local), jnp.float32)
    )
    factors = lax.psum(partial_value, "atom")
    filtered, filter_grad, virial = kterms(factors, kvec, filter_weight, grad_scale)
    filter_grad, virial = lax.psum((filter_grad, virial), "kvec")
    dims_k = (((1,), (1,)), ((), ()))
    dims_c = (((0,), (0,)), ((), ()))

    def second_pass(block_id, totals):
        feat_acc, force_acc = totals
        offset = (block_id * block_len).astype(jnp.int32)
        mill_block = lax.dynamic_slice_in_dim(miller, offset, block_len, 1)
        filt_block = lax.dynamic_slice_in_dim(filtered, offset, block_len, 2)
        kvec_block = lax.dynamic_slice_in_dim(kvec, offset, block_len, 1)
        cos_tile, sin_tile = phases(frac_pos, mill_block)
        feat_acc = (
            feat_acc
            + lax.dot_general(filt_block[2], cos_tile, dims_k, preferred_element_type=jnp.float32)
            + lax.dot_general(filt_block[3], sin_tile, dims_k, preferred_element_type=jnp.float32)
        )
        along_cos = lax.dot_general(
            stacked,
            jnp.concatenate([filt_block[3], filt_block[1]], axis=0),
            dims_c,
            preferred_element_type=jnp.float32,
        )
        along_sin = lax.dot_general(
            stacked,
            jnp.concatenate([filt_block[2], filt_block[0]], axis=0),
            dims_c,
            preferred_element_type=jnp.float32,
        )
        dphase = (
            cos_tile.astype(jnp.float32) * along_cos - sin_tile.astype(jnp.float32) * along_sin
        ) / math.sqrt(K)
        force_acc = force_acc - lax.dot_general(kvec_block, dphase, dims_k, precision=PRECISE)
        return (feat_acc, force_acc)

    start_acc = (
        jnp.zeros((channels, atoms_local), jnp.float32),
        jnp.zeros((3, atoms_local), jnp.float32),
    )
    feat_acc, force_acc = lax.fori_loop(0, block_count, second_pass, start_acc)
    feat_part = feat_acc / math.sqrt(K)
    feat_total, force_total = lax.psum((feat_part, force_acc), "kvec")
    piece_len = atoms_local // lax.axis_size("kvec")
    start_col = lax.axis_index("kvec") * piece_len
    feat_grad = lax.dynamic_slice_in_dim(feat_total, start_col, piece_len, 1)
    force = lax.dynamic_slice_in_dim(force_total, start_col, piece_len, 1)
    return (feat_grad, force, filter_grad, virial)


def solution(mesh):
    return jax.shard_map(
        per_device,
        mesh=mesh,
        in_specs=(
            P(None, "atom"),
            P("atom"),
            P(),
            P(None, "atom"),
            P(),
            P(None, "kvec"),
            P(),
            P(None, "atom"),
        ),
        out_specs=(P(None, ("atom", "kvec")), P(None, ("atom", "kvec")), P(), P()),
        check_vma=False,
    )
```

profile of v0, /device:TPU:1, one launch (start us, length us, event | category | flops | bytes accessed | tf_op | source)
XLA Modules:
  0.0 589.7 jit_solution(16753803463641218596)
XLA Ops:
  7.2 1.1 fusion.36
  9.1 12.5 %while.29 = (s32[]{:T(128)}, f32[4,64,1024]{2,1,0:T(8,128)S(1)}, f32[3,384]{1,0:T(4,128)S(1)}, s32[3,1024]{1,0:T(4,128)S(1)}, bf16[128,384]{1,0:T(8,128)(2,1)S(1...) while((s32[]{:T(128)}, f32[4,64,1024]{2,1,0:T(8,128)S(1)}, f32[3,384]{1,0:T(4,128)S(1)}, ...), condition=%wide.region_1.0_spmd, body=%wide.region_0.0_spmd.sunk | while | flops 103941632 | bytes 2873499 | solution.py:81
  9.1 3.0 convolution_bitcast_fusion.9
  12.2 3.0 convolution_bitcast_fusion.10
  15.4 3.0 convolution_bitcast_fusion.9
  18.4 3.0 convolution_bitcast_fusion.10
  21.6 1.0 copy-done.2
  23.9 442.9 %all-reduce.4.cloned.1.call-done = f32[4,64,1024]{2,1,0:T(8,128)} async-done(((f32[4,64,1024]{2,1,0:T(8,128)}), f32[4,64,1024]{2,1,0:T(8,128)}) %all-reduce.4.cloned.1.call-update) | async-done | bytes 1048592 | tf_op jit(solution)/shard_map/psum | solution.py:84
  466.9 1.3 fusion.38
  469.2 25.7 %while.30 = (s32[]{:T(128)}, f32[64,384]{1,0:T(8,128)S(1)}, f32[3,384]{1,0:T(4,128)S(1)}, bf16[4,64,1024]{2,1,0:T(8,128)(2,1)S(1)}, f32[3,384]{1,0:T(4,128)S(1)}...) while((s32[]{:T(128)}, f32[64,384]{1,0:T(8,128)S(1)}, ...), condition=%wide.region_4.0_spmd.clone, body=%wide.region_3.0_spmd.clone.sunk | while | flops 165359360 | bytes 4749066 | solution.py:124
  469.5 3.0 convolution_add_fusion.4
  472.5 3.0 convolution_add_fusion.5
  475.5 2.9 fusion.106
  478.4 3.0 fusion.107
  481.4 0.7 convolution_subtract_fusion.2
  482.3 3.0 convolution_add_fusion.4
  485.3 3.0 convolution_add_fusion.5
  488.3 2.9 fusion.106
  491.2 3.0 fusion.107
  494.2 0.7 convolution_subtract_fusion.2
  494.9 0.7 broadcast_multiply_fusion
  495.8 35.0 %all-reduce = (f32[3,384]{1,0:T(4,128)S(1)}, f32[16,64]{1,0:T(8,128)}, f32[3,3]{1,0:T(4,128)}) all-reduce(f32[3,384]{1,0:T(4,128)S(1)} %get-tuple-element.240, f32[16,64]{1,0:T(8,128)S(1)} %convolution_multiply_fusion, f32[3,3]{1,0:T(4,128)S(1)} %convolution_multiply_fusion.1), channel_id=1, replica_groups=mesh['atom'=64,'kvec'=8] {'kvec'}, use_global_device_ids=true, to_apply=%region_6.0 | all-reduce | flops 2185 | bytes 17480 | tf_op jit(solution)/shard_map/psum | solution.py:126
  531.4 49.8 %all-reduce.6.cloned.1.call-done = f32[64,384]{1,0:T(8,128)} async-done(((f32[64,384]{1,0:T(8,128)}), f32[64,384]{1,0:T(8,128)}) %all-reduce.6.cloned.1.call-update) | async-done | bytes 98320 | tf_op jit(solution)/shard_map/psum | solution.py:126
  581.2 0.9 constant_dynamic-slice_fusion.1
  (49 shorter events, 4.9 us)
Async XLA Ops:
  7.2 16.3 %copy-start = (f32[16,64]{1,0:T(8,128)S(1)}, f32[16,64]{1,0:T(8,128)}, u32[]{:S(2)}) copy-start(f32[16,64]{1,0:T(8,128)} %param.18) | copy-start | bytes 12292
  7.2 459.7 %all-reduce.4.cloned.1.call-start = ((), (), s32[]{:S(2)}) async-start(), calls=%async_computation | async-start | bytes 2097152 | tf_op jit(solution)/shard_map/psum | solution.py:84
  7.2 1.1 copy-start.5
  8.4 0.7 copy-start.3
  8.4 0.7 copy-start.4
  21.6 1.0 copy-start.2
  22.6 558.6 %all-reduce.6.cloned.1.call-start = ((), (), s32[]{:S(2)}) async-start(), calls=%async_computation.1 | async-start | bytes 196608 | tf_op jit(solution)/shard_map/psum | solution.py:126
  22.7 0.7 copy-start.6
  466.9 2.2 copy-start.1
Sparse Core Ops, SparseCore 0:
  22.8 444.0 all-reduce.3
  495.7 85.4 all-reduce.5
where the time goes:
time: 593 us; the launch traced here: 590 us
  waiting for transfers between devices  493 us (83%)
  matrix products  39.9 us (7%)
  blocking collectives  35 us (6%)
  between operations  14.2 us (2%)
    psum x1, waiting for transfers between devices, per_device(): factors = lax.psum(partial_value, 'atom')  443 us
    psum x1, waiting for transfers between devices, per_device(): feat_total, force_total = lax.psum((feat_part, force_acc), 'kvec')  49.8 us
    psum x1, blocking collectives, per_device(): feat_total, force_total = lax.psum((feat_part, force_acc), 'kvec')  35 us
  transfers between devices with their start and end apart: 2, of which 2 were waited for; matrix products, arithmetic and copies ran while one was open for 0% of the time, Pallas kernels for 0%

commit v1 on v0

v1 whole, which is shorter than its diff:
```python
import functools
import math

import jax
import jax.numpy as jnp
import numpy as np
from jax import lax
from jax.experimental import pallas as pl
from jax.experimental.pallas import tpu as pltpu
from jax.sharding import PartitionSpec as P

K = 8192
MMAX = 40
TWO_PI = 2.0 * math.pi
PRECISE = lax.Precision.HIGHEST
MESH = pl.DeviceIdType.MESH
F32, BF16 = jnp.float32, jnp.bfloat16
MAGIC = 12582912.0

NZ = 16
NX = 4
NV = 8
CH = 4
ATOMS = 384
KL = 256
PIECE = 48

NN = (((1,), (0,)), ((), ()))
NT = (((1,), (1,)), ((), ()))
TN = (((0,), (0,)), ((), ()))


def _fit(fn, degree):
    n = 64
    nodes = 0.125 + 0.125 * np.cos(np.pi * (np.arange(n) + 0.5) / n)
    cheb = np.polynomial.chebyshev.Chebyshev.fit(nodes, fn(np.sqrt(nodes)), degree, domain=[0.0, 0.25])
    return [float(c) for c in cheb.convert(kind=np.polynomial.Polynomial).coef]


ROOT2 = math.sqrt(2.0)
SIN_C = _fit(lambda r: ROOT2 * np.sin(np.pi * r) / r, 4)
COS_C = _fit(lambda r: ROOT2 * np.cos(np.pi * r), 4)


def horner(u, coef):
    acc = coef[-1] * u + coef[-2]
    for c in coef[-3::-1]:
        acc = acc * u + c
    return acc


def cos_sin_turns(t):
    r = t - ((t + MAGIC) - MAGIC)
    u = r * r
    s = r * horner(u, SIN_C)
    c = horner(u, COS_C)
    return 1.0 - s * s, s * c


def dot(a, b, dims=NN, precision=None):
    return lax.dot_general(a, b, dims, preferred_element_type=F32, precision=precision)


def iota(shape, axis):
    return lax.broadcasted_iota(jnp.int32, shape, axis)


def select(cond):
    return jnp.where(cond, 1.0, 0.0).astype(BF16)


def kernel(
    feat_ref, spec_ref, emb_ref, frac_ref, box_ref, mil_ref, w_ref, cot_ref,
    feat_out, force_out, wgrad_out, vir_out,
    gbuf, pos_s, cbuf, sbuf, tcbuf, tsbuf, tbuf, mrep, wm_s, bk_s, filt, slope, facc,
    rs_snd, rs_buf, ag_buf, pl_snd, pl_buf, zs_buf, fg_s, alc, als, dbuf, fin_snd, fin_buf,
    g_ss, g_rs, rs_ss, rs_rs, ag_ss, ag_rs, pl_ss, pl_rs, zs_ss, zs_rs, fin_ss, fin_rs,
):
    a = lax.axis_index("atom")
    v = lax.axis_index("kvec")
    y_lo = a // (2 * NZ)
    z = (a // 2) % NZ
    core = a % 2
    y_hi = v // NX
    x = v % NX
    mine = y_lo * 2 + core

    def device(yl, zz, cc, vv):
        return {"atom": (yl * NZ + zz) * 2 + cc, "kvec": vv}

    def z_peer(i):
        return device(y_lo, (z + i) % NZ, core, v)

    def plane_peer(p, q, j):
        return device((y_lo + p) % 2, z, (core + q) % 2, (v + j) % NV)

    far_first = [8, 7, 9, 6, 10, 5, 11, 4, 12, 3, 13, 2, 14, 1, 15]
    plane = [(p, q, j) for p in (1, 0) for q in (1, 0) for j in (4, 6, 2, 5, 7, 3, 1, 0)]
    plane = [t for t in plane if t != (0, 0, 0)]

    def plane_slot(p, q, j):
        return (p * 2 + q) * 8 + j

    def send(src, dst, ss, rs, dev):
        cp = pltpu.make_async_remote_copy(
            src_ref=src, dst_ref=dst, send_sem=ss, recv_sem=rs, device_id=dev, device_id_type=MESH
        )
        cp.start()
        return cp

    barrier = pltpu.get_barrier_semaphore()
    for i in far_first:
        pl.semaphore_signal(barrier, inc=1, device_id=z_peer(i), device_id_type=MESH)
    for t in plane:
        pl.semaphore_signal(barrier, inc=1, device_id=plane_peer(*t), device_id_type=MESH)

    onehot = jnp.where(spec_ref[...] == iota((4, ATOMS), 0), 1.0, 0.0)
    lookup = dot(emb_ref[...], onehot, TN, PRECISE)
    hidden = (feat_ref[...].astype(F32) + lookup).astype(BF16)
    stacked = jnp.concatenate([hidden, cot_ref[...]], axis=0)
    r128, c128 = iota((128, 128), 0), iota((128, 128), 1)
    perm = select(c128 == ((r128 // 4) % 2) * 64 + (r128 // 8) * 4 + r128 % 4)
    gbuf[mine, 0:128, :] = dot(perm, stacked).astype(BF16)
    xyz = frac_ref[...]
    hi = xyz.astype(BF16).astype(F32)
    rest = xyz - hi
    mid = rest.astype(BF16).astype(F32)
    pos_s[...] = jnp.zeros_like(pos_s)
    pos_s[0:3, :] = hi
    pos_s[3:6, :] = mid
    pos_s[6:9, :] = rest - mid
    gbuf[mine, 128:144, :] = pos_s[...].astype(BF16)

    pl.semaphore_wait(barrier, len(far_first) + len(plane))

    gathers = [
        send(gbuf.at[mine], gbuf.at[mine], g_ss.at[0], g_rs.at[0], device(y_lo, z, 1 - core, v))
    ]
    y_to = (y_hi * 2 + y_lo + 3 + 2 * core) % 4
    for c in (0, 1):
        gathers.append(
            send(
                gbuf.at[mine], gbuf.at[mine], g_ss.at[1 + c], g_rs.at[1 + core],
                device(y_to % 2, z, c, (y_to // 2) * NX + x),
            )
        )

    def gather_wait(slot, k):
        pltpu.make_async_remote_copy(
            src_ref=gbuf.at[mine], dst_ref=gbuf.at[slot], send_sem=g_ss.at[0], recv_sem=g_rs.at[k],
            device_id=device(y_lo, z, 1 - core, v), device_id_type=MESH,
        ).wait_recv()

    mill = mil_ref[:, pl.ds(pl.multiple_of(mine * KL, KL), KL)].astype(F32)
    mrep[...] = jnp.zeros_like(mrep)
    for i in range(3):
        mrep[3 * i : 3 * i + 3, :] = mill
    mrep_b = mrep[...].astype(BF16)

    def phases(slot):
        tbuf[...] = dot(gbuf[slot, 128:144, :], mrep_b, TN)

        def body(i, carry):
            rows = pl.ds(pl.multiple_of(i * 32, 32), 32)
            c, s = cos_sin_turns(tbuf[rows, :])
            cbuf[slot, rows, :] = c.astype(BF16)
            sbuf[slot, rows, :] = s.astype(BF16)
            return carry

        lax.fori_loop(0, ATOMS // 32, body, 0, unroll=2)

    def factors(slot):
        sp = gbuf[slot, 0:128, :]
        return dot(sp, cbuf[slot]), dot(sp, sbuf[slot])

    phases(mine)
    fc, fs = factors(mine)
    facc[0] = fc
    facc[1] = fs
    for k, slot in ((0, y_lo * 2 + 1 - core), (1, (1 - y_lo) * 2), (2, (1 - y_lo) * 2 + 1)):
        gather_wait(slot, k)
        phases(slot)
        fc, fs = factors(slot)
        facc[0] = facc[0] + fc
        facc[1] = facc[1] + fs
    rs_snd[:, 0:8, :] = facc[0].reshape(NZ, 8, KL)
    rs_snd[:, 8:16, :] = facc[1].reshape(NZ, 8, KL)
    rs = []
    for i in far_first:
        rs.append(send(rs_snd.at[(z + i) % NZ], rs_buf.at[i], rs_ss.at[i], rs_rs.at[i], z_peer(i)))

    kvec = TWO_PI * mill / box_ref[...]
    q_vals = jnp.sum(kvec * kvec, axis=0, keepdims=True)
    nb = w_ref.shape[0]
    q_top = 3.0 * (TWO_PI * MMAX / 105.0) ** 2
    spread = 1.5 * q_top / (nb - 1)
    centers = q_top * iota((nb, KL), 0).astype(F32) / (nb - 1)
    offsets = (q_vals - centers) / spread
    basis = jnp.exp(-offsets * offsets)
    basis_slope = -2.0 * offsets / spread * basis
    p64, c64 = iota((64, 128), 0), iota((64, 128), 1)
    spreadw = jnp.where(p64 == (c64 // 8) * 4 + c64 % 4, 1.0, 0.0)
    w2 = dot(w_ref[...], spreadw, NN, PRECISE)
    filt[...] = dot(w2, basis, TN, PRECISE).reshape(NZ, 8, KL)
    slope[...] = dot(w2, basis_slope, TN, PRECISE).reshape(NZ, 8, KL)
    bk_s[...] = jnp.zeros_like(bk_s)
    bk_s[0:16, :] = basis
    bk_s[16:19, :] = kvec
    bk_s[28:31, :] = kvec
    wm_s[...] = jnp.zeros_like(wm_s)
    for g in range(8):
        wm_s[16 * g : 16 * g + 3, :] = mill
    p, pp = iota((128, 256), 0), iota((128, 256), 1)
    d_, r_ = pp // 16, pp % 16
    source = 8 * d_ + ((r_ // 4 + 1) % 2) * 4 + r_ % 4
    pick_c = select((p == source) & (r_ >= 8))
    pick_s = select((p == source) & (r_ < 8))
    for s in range(4):
        sp = gbuf[s, 0:128, :]
        tcbuf[s] = dot(sp, pick_c, TN).astype(BF16)
        tsbuf[s] = dot(sp, pick_s, TN).astype(BF16)

    total = rs_snd[z]
    for k, i in enumerate(far_first[::-1]):
        rs[len(far_first) - 1 - k].wait_recv()
        total = total + rs_buf[i]
    total = total * (1.0 / math.sqrt(NZ * 4 * ATOMS))
    c8, s8 = total[0:8], total[8:16]
    f8 = filt[z]
    ag_buf[z] = jnp.concatenate([c8 * f8, s8 * f8], axis=0).astype(BF16)
    ag = []
    for i in far_first:
        ag.append(send(ag_buf.at[z], ag_buf.at[z], ag_ss.at[i], ag_rs.at[i], z_peer(i)))

    energy = c8 * pltpu.roll(c8, 4, 0) + s8 * pltpu.roll(s8, 4, 0)
    weight = 0.5 * jnp.sum(slope[z] * energy, axis=0, keepdims=True)
    lhs = jnp.where(iota((8, KL), 0) < 4, energy, bk_s[24:32, :] * weight)
    pl_snd[...] = dot(lhs, bk_s[...], NT, PRECISE)
    pls = []
    for t in plane:
        n = plane_slot(*t)
        pls.append(send(pl_snd, pl_buf.at[n], pl_ss.at[n], pl_rs.at[n], plane_peer(*t)))
    psum = pl_snd[...]
    for t, cp in zip(plane, pls):
        cp.wait_recv()
        psum = psum + pl_buf[plane_slot(*t)]
    zs_buf[z] = psum
    zs = []
    for i in far_first:
        zs.append(send(zs_buf.at[z], zs_buf.at[z], zs_ss.at[i], zs_rs.at[i], z_peer(i)))

    def z_wait(buf, ss, rsem, i):
        pltpu.make_async_remote_copy(
            src_ref=buf.at[z], dst_ref=buf.at[(z + NZ - i) % NZ], send_sem=ss.at[i], recv_sem=rsem.at[i],
            device_id=z_peer(i), device_id_type=MESH,
        ).wait_recv()

    for i in far_first[::-1]:
        z_wait(ag_buf, ag_ss, ag_rs, i)

    terms = ag_buf[...].reshape(256, KL)
    cc_, pp = iota((128, 256), 0) % 64, iota((128, 256), 1)
    at = (cc_ // 4) * 16 + cc_ % 4
    xx = dot(select(pp == at + 4), terms).astype(BF16)
    yy = dot(select(pp == at + 12), terms).astype(BF16)
    wm = wm_s[...].astype(BF16)
    lane = iota((8, 24, 128), 2)
    lane8 = iota((8, 8, 128), 2)
    fins = []
    for p, q in ((1, 1), (1, 0), (0, 1), (0, 0)):
        slot = ((y_lo + p) % 2) * 2 + (core + q) % 2
        alc[...] = dot(tcbuf[slot], terms)
        als[...] = dot(tsbuf[slot], terms)

        def body(i, carry):
            rows = pl.ds(pl.multiple_of(i * 32, 32), 32)
            dbuf[rows, :] = (
                cbuf[slot, rows, :].astype(F32) * alc[rows, :] - sbuf[slot, rows, :].astype(F32) * als[rows, :]
            ).astype(BF16)
            return carry

        lax.fori_loop(0, ATOMS // 32, body, 0, unroll=2)
        out_a = (dot(cbuf[slot], xx, NT) + dot(sbuf[slot], yy, NT)).reshape(NV, PIECE, 128)
        out_b = dot(dbuf[...], wm, NT).reshape(NV, PIECE, 128)
        packed = jnp.where(lane < 64, out_a[:, 0:24, :], out_a[:, 24:48, :])
        pushed = jnp.zeros((NV, 8, 128), F32)
        for g in range(6):
            pushed = jnp.where(lane8 // 16 == g, out_b[:, 8 * g : 8 * g + 8, :], pushed)
        fin_snd[slot] = jnp.concatenate([packed, pushed], axis=1).astype(BF16)
        for t in plane:
            if t[:2] == (p, q):
                n = plane_slot(*t)
                fins.append(
                    send(
                        fin_snd.at[slot, (v + t[2]) % NV], fin_buf.at[n], fin_ss.at[n], fin_rs.at[n],
                        plane_peer(*t),
                    )
                )

    for i in far_first[::-1]:
        z_wait(zs_buf, zs_ss, zs_rs, i)
    vsum = zs_buf[0]
    for d in range(NZ):
        fg_s[4 * d : 4 * d + 4, :] = zs_buf[d, 0:4, :]
        if d:
            vsum = vsum + zs_buf[d]
    grad_scale = math.sqrt(NZ * 4 * ATOMS) / math.sqrt(K)
    wgrad_out[...] = jnp.transpose(fg_s[...])[0:16, 0:64] * grad_scale
    vir_out[...] = vsum[4:7, 16:19] * (-2.0 * grad_scale)

    acc = fin_snd[mine, v].astype(F32)
    for t, cp in zip(plane, fins):
        cp.wait_recv()
        acc = acc + fin_buf[plane_slot(*t)].astype(F32)
    acc = acc * (1.0 / math.sqrt(K))
    turned = jnp.transpose(jnp.concatenate([acc, jnp.zeros((96, 128), F32)], axis=0))
    feat_out[:, 0:24] = turned[0:64, 0:24]
    feat_out[:, 24:48] = turned[64:128, 0:24]
    unit = -TWO_PI / box_ref[...]
    for g in range(6):
        force_out[:, 8 * g : 8 * g + 8] = turned[16 * g : 16 * g + 3, 24:32] * unit

    for cp in gathers + rs + ag + pls + zs + fins:
        cp.wait_send()


def per_device(features, species, embed, frac_pos, box, miller, filter_weight, cotangent):
    channels, atoms = features.shape
    assert (channels, atoms, miller.shape[1]) == (NZ * CH, ATOMS, 4 * KL)
    vmem = pl.BlockSpec(memory_space=pltpu.VMEM)
    dma = pltpu.SemaphoreType.DMA
    scratch = [
        pltpu.VMEM((4, 144, ATOMS), BF16),
        pltpu.VMEM((16, ATOMS), F32),
        pltpu.VMEM((4, ATOMS, KL), BF16),
        pltpu.VMEM((4, ATOMS, KL), BF16),
        pltpu.VMEM((4, ATOMS, KL), BF16),
        pltpu.VMEM((4, ATOMS, KL), BF16),
        pltpu.VMEM((ATOMS, KL), F32),
        pltpu.VMEM((16, KL), F32),
        pltpu.VMEM((128, KL), F32),
        pltpu.VMEM((128, KL), F32),
        pltpu.VMEM((NZ, 8, KL), F32),
        pltpu.VMEM((NZ, 8, KL), F32),
        pltpu.VMEM((2, 128, KL), F32),
        pltpu.VMEM((NZ, 16, KL), F32),
        pltpu.VMEM((NZ, 16, KL), F32),
        pltpu.VMEM((NZ, 16, KL), BF16),
        pltpu.VMEM((8, 128), F32),
        pltpu.VMEM((32, 8, 128), F32),
        pltpu.VMEM((NZ, 8, 128), F32),
        pltpu.VMEM((128, 128), F32),
        pltpu.VMEM((ATOMS, KL), F32),
        pltpu.VMEM((ATOMS, KL), F32),
        pltpu.VMEM((ATOMS, KL), BF16),
        pltpu.VMEM((4, NV, 32, 128), BF16),
        pltpu.VMEM((32, 32, 128), BF16),
        dma((3,)), dma((3,)), dma((NZ,)), dma((NZ,)), dma((NZ,)), dma((NZ,)),
        dma((32,)), dma((32,)), dma((NZ,)), dma((NZ,)), dma((32,)), dma((32,)),
    ]
    return pl.pallas_call(
        kernel,
        out_shape=(
            jax.ShapeDtypeStruct((channels, PIECE), F32),
            jax.ShapeDtypeStruct((3, PIECE), F32),
            jax.ShapeDtypeStruct(filter_weight.shape, F32),
            jax.ShapeDtypeStruct((3, 3), F32),
        ),
        in_specs=[vmem] * 8,
        out_specs=(vmem,) * 4,
        scratch_shapes=scratch,
        compiler_params=pltpu.CompilerParams(collective_id=0, has_side_effects=True),
        name="ewald",
    )(features, species[None, :], embed, frac_pos, box[:, None], miller, filter_weight, cotangent)


def solution(mesh):
    return jax.shard_map(
        per_device,
        mesh=mesh,
        in_specs=(
            P(None, "atom"), P("atom"), P(), P(None, "atom"), P(), P(None, "kvec"), P(), P(None, "atom"),
        ),
        out_specs=(P(None, ("atom", "kvec")), P(None, ("atom", "kvec")), P(), P()),
        check_vma=False,
    )
```

time: 593 us -> 64.3 us (0.11)
  waiting for transfers between devices: 493 us -> 0 us
  Pallas kernels: 0 us -> 58.2 us
  matrix products: 39.9 us -> 0 us
  blocking collectives: 35 us -> 0 us
  between operations: 14.2 us -> 0.67 us
    psum x2 -> x0, waiting for transfers between devices: 493 us -> none  [the longest x1 443 us: per_device(): factors = lax.psum(partial_value, 'atom')]
    pallas_call x0 -> x1, Pallas kernels: none -> 58.2 us  [per_device(): pl.pallas_call(kernel, out_shape=(jax.ShapeDtypeStruct((channels, PIECE),...]
    dot_general x19 -> x0, matrix products: 39.9 us -> none  [the longest x2 6.09 us: first_pass(): sin_part = jnp.dot(stacked, sin_tile, preferred_element_type=jnp.float32)]
    psum x1 -> x0, blocking collectives: 35 us -> none  [per_device(): feat_total, force_total = lax.psum((feat_part, force_acc), 'kvec')]
  transfers between devices with their start and end apart: 2 -> 0, of which waited for: 2 -> 0; matrix products, arithmetic and copies ran while one was open for 0% -> 0% of each run, Pallas kernels for 0% -> 0%
where the time goes in v1:
time: 64.3 us; the launch traced here: 64 us
  Pallas kernels  58.2 us (91%)
  local copies, waits for them, and re-layouts  5.22 us (8%)
  between operations  0.67 us (1%)
    pallas_call x1, Pallas kernels, per_device(): pl.pallas_call(kernel, out_shape=(jax.ShapeDtypeStruct((channels, PIECE),...  58.2 us
    unnamed x11, local copies, waits for them, and re-layouts  1.85 us
    pallas_call x1, local copies, waits for them, and re-layouts, per_device(): pl.pallas_call(kernel, out_shape=(jax.ShapeDtypeStruct((channels, PIECE),...  1.45 us

profile of v1, /device:TPU:1, one launch (start us, length us, event | category | flops | bytes accessed | tf_op | source)
XLA Modules:
  0.0 64.0 jit_solution(12141966834886929989)
XLA Ops:
  0.6 0.0 copy-start.3
  0.6 1.3 %broadcast_in_dim.6.spec_ref = s32[1,384]{1,0:T(1,128)} reshape(s32[384]{0:T(512)} %param.9) | data formatting | bytes 3072 | tf_op jit(solution)/shard_map/broadcast_in_dim | solution.py:374
  1.9 0.0 copy-done.3
  1.9 0.7 %copy.12.box_ref = f32[3,1]{1,0:T(4,128)} copy(f32[3,1]{0,1:T(1,128)S(1)} %bitcast.1) | data formatting | bytes 24 | tf_op jit(solution)/shard_map/broadcast_in_dim | solution.py:374
  2.6 58.2 %ewald.1 = (f32[64,48]{1,0:T(8,128)}, f32[3,48]{1,0:T(4,128)}, f32[16,64]{1,0:T(8,128)}, f32[3,3]{1,0:T(4,128)}) custom-call(bf16[64,384]{1,0:T(8,128)(2,1)} %feat_ref.1, s32[1,384]{1,0:T(1,128)} %broadcast_in_dim.6.spec_ref, f32[4,64]{1,0:T(4,128)} %emb_ref.1, f32[3,384]{1,0:T(4,128)} %frac_ref.1, f32[3,1]{1,0:T(4,128)} %copy.12.box_ref, ...), custom_call_target="tpu_custom_call" | custom-call | tf_op jit(solution)/shard_map/ewald/pallas_call | solution.py:361
  60.7 0.0 copy-start.2
  60.7 0.0 copy-start
  60.7 1.4 %copy.13 = f32[64,48]{0,1:T(8,128)} copy(f32[64,48]{1,0:T(8,128)} %get-tuple-element.4) | data formatting | bytes 24576 | tf_op jit(solution)/shard_map/ewald/pallas_call | solution.py:361
  62.2 0.0 copy-done.2
  62.2 0.6 copy.17
  62.8 0.0 copy-done
  62.8 0.0 copy-start.1
  62.8 0.6 copy.18
  63.4 0.1 copy-done.1
  63.5 0.6 copy.19
Async XLA Ops:
  0.6 1.3 %copy-start.3 = (f32[3]{0:T(128)S(1)}, f32[3]{0:T(128)}, u32[]{:S(2)}) copy-start(f32[3]{0:T(128)} %param.12) | copy-start | bytes 40
  60.7 1.5 %copy-start.2 = (f32[3,48]{1,0:T(4,128)S(1)}, f32[3,48]{1,0:T(4,128)}, u32[]{:S(2)}) copy-start(f32[3,48]{1,0:T(4,128)} %get-tuple-element.13) | copy-start | bytes 1732
  60.7 2.0 %copy-start = (f32[16,64]{1,0:T(8,128)S(1)}, f32[16,64]{1,0:T(8,128)}, u32[]{:S(2)}) copy-start(f32[16,64]{1,0:T(8,128)} %get-tuple-element.14) | copy-start | bytes 12292
  62.8 0.7 %copy-start.1 = (f32[3,3]{1,0:T(4,128)S(1)}, f32[3,3]{1,0:T(4,128)}, u32[]{:S(2)}) copy-start(f32[3,3]{1,0:T(4,128)} %get-tuple-element.15) | copy-start | bytes 112

commit v2 on v1

--- a/solution.py
+++ b/solution.py
@@ -24,6 +24,7 @@
 ATOMS = 384
 KL = 256
 PIECE = 48
+Q_TOP = 32000.0
 
 NN = (((1,), (0,)), ((), ()))
 NT = (((1,), (1,)), ((), ()))
@@ -70,12 +71,25 @@
 
 
 def kernel(
-    feat_ref, spec_ref, emb_ref, frac_ref, box_ref, mil_ref, w_ref, cot_ref,
-    feat_out, force_out, wgrad_out, vir_out,
-    gbuf, pos_s, cbuf, sbuf, tcbuf, tsbuf, tbuf, mrep, wm_s, bk_s, filt, slope, facc,
-    rs_snd, rs_buf, ag_buf, pl_snd, pl_buf, zs_buf, fg_s, alc, als, dbuf, fin_snd, fin_buf,
-    g_ss, g_rs, rs_ss, rs_rs, ag_ss, ag_rs, pl_ss, pl_rs, zs_ss, zs_rs, fin_ss, fin_rs,
+    feat_hbm, spec_hbm, emb_hbm, frac_hbm, box_ref, mil_hbm, w_hbm, cot_hbm,
+    out_ref,
+    feat_ref, spec_ref, emb_ref, frac_ref, mil_ref, w_ref, cot_ref,
+    pbuf, gbuf, pos_s, cbuf, sbuf, tcbuf, tsbuf, tbuf, mrep, wm_s, bk_s, filt, slope, facc,
+    rs_snd, rs_buf, sc_snd, sc_buf, ag_buf, pl_snd, pl_buf, zs_buf, fg_s, alc, als, dbuf, fin_snd, fin_buf,
+    in_s, p_ss, p_rs, g_ss, g_rs, rs_ss, rs_rs, sc_ss, sc_rs, ag_ss, ag_rs,
+    pl_ss, pl_rs, zs_ss, zs_rs, fin_ss, fin_rs,
 ):
+    loads = [
+        pltpu.make_async_copy(src, dst, in_s.at[n])
+        for n, (src, dst) in enumerate(
+            (
+                (frac_hbm, frac_ref), (mil_hbm, mil_ref), (spec_hbm, spec_ref), (emb_hbm, emb_ref),
+                (feat_hbm, feat_ref), (cot_hbm, cot_ref), (w_hbm, w_ref),
+            )
+        )
+    ]
+    for load in loads:
+        load.start()
     a = lax.axis_index("atom")
     v = lax.axis_index("kvec")
     y_lo = a // (2 * NZ)
@@ -114,13 +128,15 @@
     for t in plane:
         pl.semaphore_signal(barrier, inc=1, device_id=plane_peer(*t), device_id_type=MESH)
 
-    onehot = jnp.where(spec_ref[...] == iota((4, ATOMS), 0), 1.0, 0.0)
+    for load in loads:
+        load.wait()
+    onehot = jnp.where(spec_ref[...].reshape(1, ATOMS) == iota((4, ATOMS), 0), 1.0, 0.0)
     lookup = dot(emb_ref[...], onehot, TN, PRECISE)
     hidden = (feat_ref[...].astype(F32) + lookup).astype(BF16)
     stacked = jnp.concatenate([hidden, cot_ref[...]], axis=0)
     r128, c128 = iota((128, 128), 0), iota((128, 128), 1)
     perm = select(c128 == ((r128 // 4) % 2) * 64 + (r128 // 8) * 4 + r128 % 4)
-    gbuf[mine, 0:128, :] = dot(perm, stacked).astype(BF16)
+    gbuf[mine] = dot(perm, stacked).astype(BF16)
     xyz = frac_ref[...]
     hi = xyz.astype(BF16).astype(F32)
     rest = xyz - hi
@@ -129,26 +145,27 @@
     pos_s[0:3, :] = hi
     pos_s[3:6, :] = mid
     pos_s[6:9, :] = rest - mid
-    gbuf[mine, 128:144, :] = pos_s[...].astype(BF16)
+    pbuf[mine] = pos_s[...].astype(BF16)
 
     pl.semaphore_wait(barrier, len(far_first) + len(plane))
 
-    gathers = [
-        send(gbuf.at[mine], gbuf.at[mine], g_ss.at[0], g_rs.at[0], device(y_lo, z, 1 - core, v))
-    ]
     y_to = (y_hi * 2 + y_lo + 3 + 2 * core) % 4
-    for c in (0, 1):
-        gathers.append(
-            send(
-                gbuf.at[mine], gbuf.at[mine], g_ss.at[1 + c], g_rs.at[1 + core],
-                device(y_to % 2, z, c, (y_to // 2) * NX + x),
+    other = device(y_lo, z, 1 - core, v)
+    gathers = []
+    for buf, ss, rsem in ((pbuf, p_ss, p_rs), (gbuf, g_ss, g_rs)):
+        for c in (0, 1):
+            gathers.append(
+                send(
+                    buf.at[mine], buf.at[mine], ss.at[1 + c], rsem.at[1 + core],
+                    device(y_to % 2, z, c, (y_to // 2) * NX + x),
+                )
             )
-        )
-
-    def gather_wait(slot, k):
+        gathers.append(send(buf.at[mine], buf.at[mine], ss.at[0], rsem.at[0], other))
+
+    def gather_wait(buf, ss, rsem, slot, k):
         pltpu.make_async_remote_copy(
-            src_ref=gbuf.at[mine], dst_ref=gbuf.at[slot], send_sem=g_ss.at[0], recv_sem=g_rs.at[k],
-            device_id=device(y_lo, z, 1 - core, v), device_id_type=MESH,
+            src_ref=buf.at[mine], dst_ref=buf.at[slot], send_sem=ss.at[0], recv_sem=rsem.at[k],
+            device_id=other, device_id_type=MESH,
         ).wait_recv()
 
     mill = mil_ref[:, pl.ds(pl.multiple_of(mine * KL, KL), KL)].astype(F32)
@@ -158,7 +175,7 @@
     mrep_b = mrep[...].astype(BF16)
 
     def phases(slot):
-        tbuf[...] = dot(gbuf[slot, 128:144, :], mrep_b, TN)
+        tbuf[...] = dot(pbuf[slot], mrep_b, TN)
 
         def body(i, carry):
             rows = pl.ds(pl.multiple_of(i * 32, 32), 32)
@@ -170,26 +187,38 @@
         lax.fori_loop(0, ATOMS // 32, body, 0, unroll=2)
 
     def factors(slot):
-        sp = gbuf[slot, 0:128, :]
+        sp = gbuf[slot]
         return dot(sp, cbuf[slot]), dot(sp, sbuf[slot])
 
     phases(mine)
+    others = ((0, y_lo * 2 + 1 - core), (1, (1 - y_lo) * 2), (2, (1 - y_lo) * 2 + 1))
     fc, fs = factors(mine)
-    facc[0] = fc
-    facc[1] = fs
-    for k, slot in ((0, y_lo * 2 + 1 - core), (1, (1 - y_lo) * 2), (2, (1 - y_lo) * 2 + 1)):
-        gather_wait(slot, k)
+    for k, slot in others:
+        gather_wait(pbuf, p_ss, p_rs, slot, k)
         phases(slot)
-        fc, fs = factors(slot)
-        facc[0] = facc[0] + fc
-        facc[1] = facc[1] + fs
-    rs_snd[:, 0:8, :] = facc[0].reshape(NZ, 8, KL)
-    rs_snd[:, 8:16, :] = facc[1].reshape(NZ, 8, KL)
+    for k, slot in others:
+        gather_wait(gbuf, g_ss, g_rs, slot, k)
+        fck, fsk = factors(slot)
+        fc = fc + fck
+        fs = fs + fsk
+    facc[0] = fc.reshape(NZ, 8, KL)
+    facc[1] = fs.reshape(NZ, 8, KL)
+    top = jnp.maximum(jnp.max(jnp.maximum(jnp.abs(fc), jnp.abs(fs)), axis=(0, 1), keepdims=True), 1e-30)
+    factor = Q_TOP / top
+
+    def coded(part):
+        return ((part * factor + MAGIC) - MAGIC).astype(jnp.int32).reshape(NZ, 8, KL)
+
+    rs_snd[...] = jnp.concatenate([coded(fc), coded(fs)], axis=1).astype(jnp.int16)
+    sc_snd[...] = jnp.broadcast_to(top * (1.0 / Q_TOP), (1, 128))
     rs = []
     for i in far_first:
+        rs.append(send(sc_snd, sc_buf.at[i], sc_ss.at[i], sc_rs.at[i], z_peer(i)))
         rs.append(send(rs_snd.at[(z + i) % NZ], rs_buf.at[i], rs_ss.at[i], rs_rs.at[i], z_peer(i)))
 
-    kvec = TWO_PI * mill / box_ref[...]
+    row3 = iota((3, 1), 0)
+    box = jnp.where(row3 == 0, box_ref[0], jnp.where(row3 == 1, box_ref[1], box_ref[2]))
+    kvec = TWO_PI * mill / box
     q_vals = jnp.sum(kvec * kvec, axis=0, keepdims=True)
     nb = w_ref.shape[0]
     q_top = 3.0 * (TWO_PI * MMAX / 105.0) ** 2
@@ -216,14 +245,17 @@
     pick_c = select((p == source) & (r_ >= 8))
     pick_s = select((p == source) & (r_ < 8))
     for s in range(4):
-        sp = gbuf[s, 0:128, :]
+        sp = gbuf[s]
         tcbuf[s] = dot(sp, pick_c, TN).astype(BF16)
         tsbuf[s] = dot(sp, pick_s, TN).astype(BF16)
 
-    total = rs_snd[z]
-    for k, i in enumerate(far_first[::-1]):
-        rs[len(far_first) - 1 - k].wait_recv()
-        total = total + rs_buf[i]
+    total = jnp.concatenate([facc[0, z], facc[1, z]], axis=0)
+    for k in range(len(far_first) - 1, -1, -1):
+        i = far_first[k]
+        rs[2 * k].wait_recv()
+        rs[2 * k + 1].wait_recv()
+        step = jnp.concatenate([sc_buf[i], sc_buf[i]], axis=1)
+        total = total + rs_buf[i].astype(jnp.int32).astype(F32) * step
     total = total * (1.0 / math.sqrt(NZ * 4 * ATOMS))
     c8, s8 = total[0:8], total[8:16]
     f8 = filt[z]
@@ -305,32 +337,52 @@
         if d:
             vsum = vsum + zs_buf[d]
     grad_scale = math.sqrt(NZ * 4 * ATOMS) / math.sqrt(K)
-    wgrad_out[...] = jnp.transpose(fg_s[...])[0:16, 0:64] * grad_scale
-    vir_out[...] = vsum[4:7, 16:19] * (-2.0 * grad_scale)
+    out_ref[32:48, :] = jnp.transpose(fg_s[...])[0:16, :] * grad_scale
+    out_ref[48:56, :] = vsum * (-2.0 * grad_scale)
 
     acc = fin_snd[mine, v].astype(F32)
     for t, cp in zip(plane, fins):
         cp.wait_recv()
         acc = acc + fin_buf[plane_slot(*t)].astype(F32)
-    acc = acc * (1.0 / math.sqrt(K))
-    turned = jnp.transpose(jnp.concatenate([acc, jnp.zeros((96, 128), F32)], axis=0))
-    feat_out[:, 0:24] = turned[0:64, 0:24]
-    feat_out[:, 24:48] = turned[64:128, 0:24]
-    unit = -TWO_PI / box_ref[...]
-    for g in range(6):
-        force_out[:, 8 * g : 8 * g + 8] = turned[16 * g : 16 * g + 3, 24:32] * unit
+    unit = jnp.zeros((8, 128), F32)
+    for i in range(3):
+        unit = jnp.where(iota((8, 128), 1) % 16 == i, -TWO_PI / math.sqrt(K) / box_ref[i], unit)
+    out_ref[0:24, :] = acc[0:24] * (1.0 / math.sqrt(K))
+    out_ref[24:32, :] = acc[24:32] * unit
 
     for cp in gathers + rs + ag + pls + zs + fins:
         cp.wait_send()
+
+
+def unpack(packed_ref, feat_hbm, force_hbm, wgrad_hbm, vir_hbm, feat_s, force_s, wgrad_s, vir_s, sem):
+    wgrad_s[...] = packed_ref[32:48, 0:64]
+    vir_s[...] = packed_ref[52:55, 16:19]
+    turned = jnp.transpose(packed_ref[...])
+    feat_s[:, 0:24] = turned[0:64, 0:24]
+    feat_s[:, 24:48] = turned[64:128, 0:24]
+    for g in range(6):
+        force_s[:, 8 * g : 8 * g + 8] = turned[16 * g : 16 * g + 3, 24:32]
+    stores = [
+        pltpu.make_async_copy(src, dst, sem.at[n])
+        for n, (src, dst) in enumerate(
+            ((feat_s, feat_hbm), (force_s, force_hbm), (wgrad_s, wgrad_hbm), (vir_s, vir_hbm))
+        )
+    ]
+    for store in stores:
+        store.start()
+    for store in stores:
+        store.wait()
 
 
 def per_device(features, species, embed, frac_pos, box, miller, filter_weight, cotangent):
     channels, atoms = features.shape
     assert (channels, atoms, miller.shape[1]) == (NZ * CH, ATOMS, 4 * KL)
-    vmem = pl.BlockSpec(memory_space=pltpu.VMEM)
+    vmem, anywhere, smem = (pl.BlockSpec(memory_space=m) for m in (pltpu.VMEM, pl.ANY, pltpu.SMEM))
     dma = pltpu.SemaphoreType.DMA
-    scratch = [
-        pltpu.VMEM((4, 144, ATOMS), BF16),
+    loaded = [features, species, embed, frac_pos, miller, filter_weight, cotangent]
+    scratch = [pltpu.VMEM(arg.shape, arg.dtype) for arg in loaded] + [
+        pltpu.VMEM((4, 16, ATOMS), BF16),
+        pltpu.VMEM((4, 128, ATOMS), BF16),
         pltpu.VMEM((16, ATOMS), F32),
         pltpu.VMEM((4, ATOMS, KL), BF16),
         pltpu.VMEM((4, ATOMS, KL), BF16),
@@ -342,9 +394,11 @@
         pltpu.VMEM((128, KL), F32),
         pltpu.VMEM((NZ, 8, KL), F32),
         pltpu.VMEM((NZ, 8, KL), F32),
-        pltpu.VMEM((2, 128, KL), F32),
-        pltpu.VMEM((NZ, 16, KL), F32),
-        pltpu.VMEM((NZ, 16, KL), F32),
+        pltpu.VMEM((2, NZ, 8, KL), F32),
+        pltpu.VMEM((NZ, 16, KL), jnp.int16),
+        pltpu.VMEM((NZ, 16, KL), jnp.int16),
+        pltpu.VMEM((1, 128), F32),
+        pltpu.VMEM((NZ, 1, 128), F32),
         pltpu.VMEM((NZ, 16, KL), BF16),
         pltpu.VMEM((8, 128), F32),
         pltpu.VMEM((32, 8, 128), F32),
@@ -355,23 +409,31 @@
         pltpu.VMEM((ATOMS, KL), BF16),
         pltpu.VMEM((4, NV, 32, 128), BF16),
         pltpu.VMEM((32, 32, 128), BF16),
-        dma((3,)), dma((3,)), dma((NZ,)), dma((NZ,)), dma((NZ,)), dma((NZ,)),
+        dma((7,)), dma((3,)), dma((3,)), dma((3,)), dma((3,)),
+        dma((NZ,)), dma((NZ,)), dma((NZ,)), dma((NZ,)), dma((NZ,)), dma((NZ,)),
         dma((32,)), dma((32,)), dma((NZ,)), dma((NZ,)), dma((32,)), dma((32,)),
     ]
-    return pl.pallas_call(
+    packed = pl.pallas_call(
         kernel,
-        out_shape=(
-            jax.ShapeDtypeStruct((channels, PIECE), F32),
-            jax.ShapeDtypeStruct((3, PIECE), F32),
-            jax.ShapeDtypeStruct(filter_weight.shape, F32),
-            jax.ShapeDtypeStruct((3, 3), F32),
-        ),
-        in_specs=[vmem] * 8,
-        out_specs=(vmem,) * 4,
+        out_shape=jax.ShapeDtypeStruct((128, 128), F32),
+        in_specs=[anywhere] * 4 + [smem] + [anywhere] * 3,
+        out_specs=vmem,
         scratch_shapes=scratch,
         compiler_params=pltpu.CompilerParams(collective_id=0, has_side_effects=True),
         name="ewald",
-    )(features, species[None, :], embed, frac_pos, box[:, None], miller, filter_weight, cotangent)
+    )(features, species, embed, frac_pos, box, miller, filter_weight, cotangent)
+    results = [
+        jax.ShapeDtypeStruct(shape, F32)
+        for shape in ((channels, PIECE), (3, PIECE), filter_weight.shape, (3, 3))
+    ]
+    return pl.pallas_call(
+        unpack,
+        out_shape=results,
+        in_specs=[vmem],
+        out_specs=[anywhere] * 4,
+        scratch_shapes=[pltpu.VMEM(r.shape, F32) for r in results] + [dma((4,))],
+        name="unpack",
+    )(packed)
 
 
 def solution(mesh):

time: 64.3 us -> 56.9 us (0.88)
  local copies, waits for them, and re-layouts: 5.22 us -> 1.44 us
  Pallas kernels: 58.2 us -> 54.5 us
    pallas_call x1 -> x2, Pallas kernels: 58.2 us -> 54.5 us  [the longest x1 52.9 us: per_device(): pl.pallas_call(kernel, out_shape=jax.ShapeDtypeStruct((128, 128), F32), i...]
    broadcast_in_dim x2 -> x0, local copies, waits for them, and re-layouts: 1.91 us -> none  [the longest x1 1.25 us: per_device(): species[None, :]]
    unnamed x11 -> x0, local copies, waits for them, and re-layouts: 1.85 us -> none
where the time goes in v2:
time: 56.9 us; the launch traced here: 56.6 us
  Pallas kernels  54.5 us (96%)
  local copies, waits for them, and re-layouts  1.44 us (3%)
  between operations  0.65 us (1%)
    pallas_call x1, Pallas kernels, per_device(): pl.pallas_call(kernel, out_shape=jax.ShapeDtypeStruct((128, 128), F32), i...  52.9 us
    pallas_call x1, Pallas kernels, per_device(): pl.pallas_call(unpack, out_shape=results, in_specs=[vmem], out_specs=[any...  1.66 us
    pallas_call x1, local copies, waits for them, and re-layouts, per_device(): pl.pallas_call(unpack, out_shape=results, in_specs=[vmem], out_specs=[any...  1.44 us

profile of v2, /device:TPU:1, one launch (start us, length us, event | category | flops | bytes accessed | tf_op | source)
XLA Modules:
  0.0 56.6 jit_solution(15682641891025578136)
XLA Ops:
  0.6 52.9 %ewald.1.packed_ref = f32[128,128]{1,0:T(8,128)} custom-call(bf16[64,384]{1,0:T(8,128)(2,1)} %feat_hbm.1, s32[384]{0:T(512)} %spec_hbm.1, f32[4,64]{1,0:T(4,128)} %emb_hbm.1, f32[3,384]{1,0:T(4,128)} %frac_hbm.1, f32[3]{0:T(128)} %box_ref.1, s32[3,1024]{1,0:T(4,128)} %mil_hbm.1, f32[16,64]{1,0:T(8,128)} %w_hbm.1, bf16[64,384]{1,0:T(8,128)(2,1)} %cot_hbm.1), custom_call_target="tpu_custom_call" | custom-call | tf_op jit(solution)/shard_map/ewald/pallas_call | solution.py:416
  53.5 1.7 %unpack.1 = (f32[64,48]{1,0:T(8,128)}, f32[3,48]{1,0:T(4,128)}, f32[16,64]{1,0:T(8,128)}, f32[3,3]{1,0:T(4,128)}) custom-call(f32[128,128]{1,0:T(8,128)} %ewald.1.packed_ref), custom_call_target="tpu_custom_call" | custom-call | tf_op jit(solution)/shard_map/unpack/pallas_call | solution.py:429
  55.2 1.4 %copy.12 = f32[64,48]{0,1:T(8,128)} copy(f32[64,48]{1,0:T(8,128)} %get-tuple-element.4) | data formatting | bytes 24576 | tf_op jit(solution)/shard_map/unpack/pallas_call | solution.py:429

commit v3 on v2

--- a/solution.py
+++ b/solution.py
@@ -71,20 +71,20 @@
 
 
 def kernel(
-    feat_hbm, spec_hbm, emb_hbm, frac_hbm, box_ref, mil_hbm, w_hbm, cot_hbm,
+    feat_hbm, spec_hbm, emb_hbm, frac_hbm, box_hbm, mil_hbm, w_hbm, cot_hbm,
     out_ref,
-    feat_ref, spec_ref, emb_ref, frac_ref, mil_ref, w_ref, cot_ref,
+    feat_ref, spec_ref, emb_ref, frac_ref, mil_ref, w_ref, cot_ref, box_ref,
     pbuf, gbuf, pos_s, cbuf, sbuf, tcbuf, tsbuf, tbuf, mrep, wm_s, bk_s, filt, slope, facc,
-    rs_snd, rs_buf, sc_snd, sc_buf, ag_buf, pl_snd, pl_buf, zs_buf, fg_s, alc, als, dbuf, fin_snd, fin_buf,
+    rs_snd, rs_buf, sc_snd, sc_buf, ag_buf, pl_snd, pl_buf, zs_buf, kv_s, alc, als, dbuf, fin_snd, fin_buf,
     in_s, p_ss, p_rs, g_ss, g_rs, rs_ss, rs_rs, sc_ss, sc_rs, ag_ss, ag_rs,
-    pl_ss, pl_rs, zs_ss, zs_rs, fin_ss, fin_rs,
+    pl_ss, pl_rs, zs_ss, zs_rs, fin_ss, fin_rs, know,
 ):
     loads = [
         pltpu.make_async_copy(src, dst, in_s.at[n])
         for n, (src, dst) in enumerate(
             (
                 (frac_hbm, frac_ref), (mil_hbm, mil_ref), (spec_hbm, spec_ref), (emb_hbm, emb_ref),
-                (feat_hbm, feat_ref), (cot_hbm, cot_ref), (w_hbm, w_ref),
+                (feat_hbm, feat_ref), (cot_hbm, cot_ref), (w_hbm, w_ref), (box_hbm, box_ref),
             )
         )
     ]
@@ -122,21 +122,25 @@
         cp.start()
         return cp
 
+    def y_peer(dy, c):
+        yy = (y_hi * 2 + y_lo + dy) % 4
+        return device(yy % 2, z, c, (yy // 2) * NX + x)
+
+    def x_peer(dx):
+        return device(y_lo, z, core, y_hi * NX + (x + dx) % NX)
+
+    def signal(sem, *devices):
+        for dev in devices:
+            pl.semaphore_signal(sem, inc=1, device_id=dev, device_id_type=MESH)
+
+    other = device(y_lo, z, 1 - core, v)
     barrier = pltpu.get_barrier_semaphore()
-    for i in far_first:
-        pl.semaphore_signal(barrier, inc=1, device_id=z_peer(i), device_id_type=MESH)
-    for t in plane:
-        pl.semaphore_signal(barrier, inc=1, device_id=plane_peer(*t), device_id_type=MESH)
-
-    for load in loads:
-        load.wait()
-    onehot = jnp.where(spec_ref[...].reshape(1, ATOMS) == iota((4, ATOMS), 0), 1.0, 0.0)
-    lookup = dot(emb_ref[...], onehot, TN, PRECISE)
-    hidden = (feat_ref[...].astype(F32) + lookup).astype(BF16)
-    stacked = jnp.concatenate([hidden, cot_ref[...]], axis=0)
-    r128, c128 = iota((128, 128), 0), iota((128, 128), 1)
-    perm = select(c128 == ((r128 // 4) % 2) * 64 + (r128 // 8) * 4 + r128 % 4)
-    gbuf[mine] = dot(perm, stacked).astype(BF16)
+    signal(
+        barrier, other, y_peer(1, 0), y_peer(1, 1), y_peer(3, 0), y_peer(3, 1),
+        x_peer(1), x_peer(3), z_peer(1), z_peer(15),
+    )
+
+    loads[0].wait()
     xyz = frac_ref[...]
     hi = xyz.astype(BF16).astype(F32)
     rest = xyz - hi
@@ -146,20 +150,15 @@
     pos_s[3:6, :] = mid
     pos_s[6:9, :] = rest - mid
     pbuf[mine] = pos_s[...].astype(BF16)
-
-    pl.semaphore_wait(barrier, len(far_first) + len(plane))
-
-    y_to = (y_hi * 2 + y_lo + 3 + 2 * core) % 4
-    other = device(y_lo, z, 1 - core, v)
+    for load in loads[1:]:
+        load.wait()
+
+    y_to = 3 + 2 * core
     gathers = []
-    for buf, ss, rsem in ((pbuf, p_ss, p_rs), (gbuf, g_ss, g_rs)):
+
+    def gather_send(buf, ss, rsem):
         for c in (0, 1):
-            gathers.append(
-                send(
-                    buf.at[mine], buf.at[mine], ss.at[1 + c], rsem.at[1 + core],
-                    device(y_to % 2, z, c, (y_to // 2) * NX + x),
-                )
-            )
+            gathers.append(send(buf.at[mine], buf.at[mine], ss.at[1 + c], rsem.at[1 + core], y_peer(y_to, c)))
         gathers.append(send(buf.at[mine], buf.at[mine], ss.at[0], rsem.at[0], other))
 
     def gather_wait(buf, ss, rsem, slot, k):
@@ -167,6 +166,20 @@
             src_ref=buf.at[mine], dst_ref=buf.at[slot], send_sem=ss.at[0], recv_sem=rsem.at[k],
             device_id=other, device_id_type=MESH,
         ).wait_recv()
+
+    pl.semaphore_wait(barrier, 9)
+    gather_send(pbuf, p_ss, p_rs)
+    signal(know.at[0], y_peer(1, core), y_peer(3, core))
+    signal(know.at[3], z_peer(1), z_peer(15))
+
+    onehot = jnp.where(spec_ref[...].reshape(1, ATOMS) == iota((4, ATOMS), 0), 1.0, 0.0)
+    lookup = dot(emb_ref[...], onehot, TN, PRECISE)
+    hidden = (feat_ref[...].astype(F32) + lookup).astype(BF16)
+    stacked = jnp.concatenate([hidden, cot_ref[...]], axis=0)
+    r128, c128 = iota((128, 128), 0), iota((128, 128), 1)
+    perm = select(c128 == ((r128 // 4) % 2) * 64 + (r128 % 4) * NZ + r128 // 8)
+    gbuf[mine] = dot(perm, stacked).astype(BF16)
+    gather_send(gbuf, g_ss, g_rs)
 
     mill = mil_ref[:, pl.ds(pl.multiple_of(mine * KL, KL), KL)].astype(F32)
     mrep[...] = jnp.zeros_like(mrep)
@@ -193,9 +206,19 @@
     phases(mine)
     others = ((0, y_lo * 2 + 1 - core), (1, (1 - y_lo) * 2), (2, (1 - y_lo) * 2 + 1))
     fc, fs = factors(mine)
+    pl.semaphore_wait(know.at[0], 2)
+    signal(know.at[1], x_peer(1), x_peer(3))
+    pl.semaphore_wait(know.at[3], 2)
+    signal(know.at[4], z_peer(2), z_peer(14))
     for k, slot in others:
         gather_wait(pbuf, p_ss, p_rs, slot, k)
         phases(slot)
+        if k == 0:
+            pl.semaphore_wait(know.at[1], 2)
+            signal(know.at[2], x_peer(1), x_peer(3))
+        if k == 1:
+            pl.semaphore_wait(know.at[4], 2)
+            signal(know.at[5], z_peer(4), z_peer(12))
     for k, slot in others:
         gather_wait(gbuf, g_ss, g_rs, slot, k)
         fck, fsk = factors(slot)
@@ -211,6 +234,7 @@
 
     rs_snd[...] = jnp.concatenate([coded(fc), coded(fs)], axis=1).astype(jnp.int16)
     sc_snd[...] = jnp.broadcast_to(top * (1.0 / Q_TOP), (1, 128))
+    pl.semaphore_wait(know.at[5], 2)
     rs = []
     for i in far_first:
         rs.append(send(sc_snd, sc_buf.at[i], sc_ss.at[i], sc_rs.at[i], z_peer(i)))
@@ -228,14 +252,17 @@
     basis = jnp.exp(-offsets * offsets)
     basis_slope = -2.0 * offsets / spread * basis
     p64, c64 = iota((64, 128), 0), iota((64, 128), 1)
-    spreadw = jnp.where(p64 == (c64 // 8) * 4 + c64 % 4, 1.0, 0.0)
+    spreadw = jnp.where(p64 == (c64 % 4) * NZ + c64 // 8, 1.0, 0.0)
     w2 = dot(w_ref[...], spreadw, NN, PRECISE)
     filt[...] = dot(w2, basis, TN, PRECISE).reshape(NZ, 8, KL)
     slope[...] = dot(w2, basis_slope, TN, PRECISE).reshape(NZ, 8, KL)
     bk_s[...] = jnp.zeros_like(bk_s)
-    bk_s[0:16, :] = basis
-    bk_s[16:19, :] = kvec
-    bk_s[28:31, :] = kvec
+    for r in range(CH):
+        bk_s[16 * r : 16 * r + 16, :] = basis
+    for r in range(3):
+        bk_s[64 + 16 * r : 67 + 16 * r, :] = kvec
+    kv_s[...] = jnp.zeros_like(kv_s)
+    kv_s[4:7, :] = kvec
     wm_s[...] = jnp.zeros_like(wm_s)
     for g in range(8):
         wm_s[16 * g : 16 * g + 3, :] = mill
@@ -266,8 +293,11 @@
 
     energy = c8 * pltpu.roll(c8, 4, 0) + s8 * pltpu.roll(s8, 4, 0)
     weight = 0.5 * jnp.sum(slope[z] * energy, axis=0, keepdims=True)
-    lhs = jnp.where(iota((8, KL), 0) < 4, energy, bk_s[24:32, :] * weight)
-    pl_snd[...] = dot(lhs, bk_s[...], NT, PRECISE)
+    lhs = jnp.where(iota((8, KL), 0) < 4, energy, kv_s[...] * weight)
+    products = dot(lhs, bk_s[...], NT, PRECISE)
+    owner = iota((8, 128), 1) // 16 == iota((8, 128), 0)
+    pl_snd[...] = jnp.sum(jnp.where(owner, products, 0.0), axis=0, keepdims=True)
+    pl.semaphore_wait(know.at[2], 2)
     pls = []
     for t in plane:
         n = plane_slot(*t)
@@ -292,7 +322,7 @@
 
     terms = ag_buf[...].reshape(256, KL)
     cc_, pp = iota((128, 256), 0) % 64, iota((128, 256), 1)
-    at = (cc_ // 4) * 16 + cc_ % 4
+    at = (cc_ % NZ) * 16 + cc_ // NZ
     xx = dot(select(pp == at + 4), terms).astype(BF16)
     yy = dot(select(pp == at + 12), terms).astype(BF16)
     wm = wm_s[...].astype(BF16)
@@ -331,14 +361,10 @@
 
     for i in far_first[::-1]:
         z_wait(zs_buf, zs_ss, zs_rs, i)
-    vsum = zs_buf[0]
+    grad_scale = math.sqrt(NZ * 4 * ATOMS) / math.sqrt(K)
+    scales = jnp.where(iota((1, 128), 1) < 64, grad_scale, -2.0 * grad_scale)
     for d in range(NZ):
-        fg_s[4 * d : 4 * d + 4, :] = zs_buf[d, 0:4, :]
-        if d:
-            vsum = vsum + zs_buf[d]
-    grad_scale = math.sqrt(NZ * 4 * ATOMS) / math.sqrt(K)
-    out_ref[32:48, :] = jnp.transpose(fg_s[...])[0:16, :] * grad_scale
-    out_ref[48:56, :] = vsum * (-2.0 * grad_scale)
+        out_ref[32 + d : 33 + d, :] = zs_buf[d] * scales
 
     acc = fin_snd[mine, v].astype(F32)
     for t, cp in zip(plane, fins):
@@ -355,13 +381,17 @@
 
 
 def unpack(packed_ref, feat_hbm, force_hbm, wgrad_hbm, vir_hbm, feat_s, force_s, wgrad_s, vir_s, sem):
-    wgrad_s[...] = packed_ref[32:48, 0:64]
-    vir_s[...] = packed_ref[52:55, 16:19]
-    turned = jnp.transpose(packed_ref[...])
-    feat_s[:, 0:24] = turned[0:64, 0:24]
-    feat_s[:, 24:48] = turned[64:128, 0:24]
+    packed = packed_ref[...]
+    feat_s[0:24, :] = packed[0:24, 0:64]
+    feat_s[24:48, :] = packed[0:24, 64:128]
+    turned = jnp.transpose(jnp.concatenate([packed, jnp.zeros((80, 128), F32)], axis=0))
     for g in range(6):
         force_s[:, 8 * g : 8 * g + 8] = turned[16 * g : 16 * g + 3, 24:32]
+    for r in range(CH):
+        wgrad_s[:, NZ * r : NZ * r + NZ] = turned[16 * r : 16 * r + 16, 32:48]
+    whole = jnp.sum(packed[32:48], axis=0, keepdims=True)
+    for r in range(3):
+        vir_s[r : r + 1, :] = whole[:, 64 + 16 * r : 67 + 16 * r]
     stores = [
         pltpu.make_async_copy(src, dst, sem.at[n])
         for n, (src, dst) in enumerate(
@@ -377,10 +407,11 @@
 def per_device(features, species, embed, frac_pos, box, miller, filter_weight, cotangent):
     channels, atoms = features.shape
     assert (channels, atoms, miller.shape[1]) == (NZ * CH, ATOMS, 4 * KL)
-    vmem, anywhere, smem = (pl.BlockSpec(memory_space=m) for m in (pltpu.VMEM, pl.ANY, pltpu.SMEM))
+    vmem, hbm, anywhere = (pl.BlockSpec(memory_space=m) for m in (pltpu.VMEM, pl.ANY, pl.ANY))
     dma = pltpu.SemaphoreType.DMA
     loaded = [features, species, embed, frac_pos, miller, filter_weight, cotangent]
     scratch = [pltpu.VMEM(arg.shape, arg.dtype) for arg in loaded] + [
+        pltpu.SMEM(box.shape, F32),
         pltpu.VMEM((4, 16, ATOMS), BF16),
         pltpu.VMEM((4, 128, ATOMS), BF16),
         pltpu.VMEM((16, ATOMS), F32),
@@ -400,23 +431,24 @@
         pltpu.VMEM((1, 128), F32),
         pltpu.VMEM((NZ, 1, 128), F32),
         pltpu.VMEM((NZ, 16, KL), BF16),
-        pltpu.VMEM((8, 128), F32),
-        pltpu.VMEM((32, 8, 128), F32),
-        pltpu.VMEM((NZ, 8, 128), F32),
-        pltpu.VMEM((128, 128), F32),
+        pltpu.VMEM((1, 128), F32),
+        pltpu.VMEM((32, 1, 128), F32),
+        pltpu.VMEM((NZ, 1, 128), F32),
+        pltpu.VMEM((8, KL), F32),
         pltpu.VMEM((ATOMS, KL), F32),
         pltpu.VMEM((ATOMS, KL), F32),
         pltpu.VMEM((ATOMS, KL), BF16),
         pltpu.VMEM((4, NV, 32, 128), BF16),
         pltpu.VMEM((32, 32, 128), BF16),
-        dma((7,)), dma((3,)), dma((3,)), dma((3,)), dma((3,)),
+        dma((8,)), dma((3,)), dma((3,)), dma((3,)), dma((3,)),
         dma((NZ,)), dma((NZ,)), dma((NZ,)), dma((NZ,)), dma((NZ,)), dma((NZ,)),
         dma((32,)), dma((32,)), dma((NZ,)), dma((NZ,)), dma((32,)), dma((32,)),
+        pltpu.SemaphoreType.REGULAR((6,)),
     ]
     packed = pl.pallas_call(
         kernel,
-        out_shape=jax.ShapeDtypeStruct((128, 128), F32),
-        in_specs=[anywhere] * 4 + [smem] + [anywhere] * 3,
+        out_shape=jax.ShapeDtypeStruct((48, 128), F32),
+        in_specs=[hbm] * 8,
         out_specs=vmem,
         scratch_shapes=scratch,
         compiler_params=pltpu.CompilerParams(collective_id=0, has_side_effects=True),
@@ -424,9 +456,9 @@
     )(features, species, embed, frac_pos, box, miller, filter_weight, cotangent)
     results = [
         jax.ShapeDtypeStruct(shape, F32)
-        for shape in ((channels, PIECE), (3, PIECE), filter_weight.shape, (3, 3))
+        for shape in ((PIECE, channels), (3, PIECE), filter_weight.shape, (3, 3))
     ]
-    return pl.pallas_call(
+    feat_grad, force, wgrad, virial = pl.pallas_call(
         unpack,
         out_shape=results,
         in_specs=[vmem],
@@ -434,6 +466,7 @@
         scratch_shapes=[pltpu.VMEM(r.shape, F32) for r in results] + [dma((4,))],
         name="unpack",
     )(packed)
+    return feat_grad.T, force, wgrad, virial
 
 
 def solution(mesh):

time: 56.9 us -> 49.8 us (0.88)
  Pallas kernels: 54.5 us -> 48.9 us
  local copies, waits for them, and re-layouts: 1.44 us -> 0 us
    pallas_call x1, Pallas kernels: 52.9 us -> 47.3 us  [per_device(): pl.pallas_call(kernel, out_shape=jax.ShapeDtypeStruct((48, 128), F32), in...]
    pallas_call x1 -> x0, local copies, waits for them, and re-layouts: 1.44 us -> none  [per_device(): pl.pallas_call(unpack, out_shape=results, in_specs=[vmem], out_specs=[any...]
where the time goes in v3:
time: 49.8 us; the launch traced here: 49.5 us
  Pallas kernels  48.9 us (98%)
  between operations  0.64 us (1%)
    pallas_call x1, Pallas kernels, per_device(): pl.pallas_call(kernel, out_shape=jax.ShapeDtypeStruct((48, 128), F32), in...  47.3 us
    pallas_call x1, Pallas kernels, per_device(): pl.pallas_call(unpack, out_shape=results, in_specs=[vmem], out_specs=[any...  1.53 us

profile of v3, /device:TPU:1, one launch (start us, length us, event | category | flops | bytes accessed | tf_op | source)
XLA Modules:
  0.0 49.5 jit_solution(5858309823705728533)
XLA Ops:
  0.6 47.3 %ewald.1.packed_ref = f32[48,128]{1,0:T(8,128)} custom-call(bf16[64,384]{1,0:T(8,128)(2,1)} %feat_hbm.1, s32[384]{0:T(512)} %spec_hbm.1, f32[4,64]{1,0:T(4,128)} %emb_hbm.1, f32[3,384]{1,0:T(4,128)} %frac_hbm.1, f32[3]{0:T(128)} %box_hbm.1, s32[3,1024]{1,0:T(4,128)} %mil_hbm.1, f32[16,64]{1,0:T(8,128)} %w_hbm.1, bf16[64,384]{1,0:T(8,128)(2,1)} %cot_hbm.1), custom_call_target="tpu_custom_call" | custom-call | tf_op jit(solution)/shard_map/ewald/pallas_call | solution.py:448
  48.0 1.5 %unpack.1 = (f32[48,64]{1,0:T(8,128)}, f32[3,48]{1,0:T(4,128)}, f32[16,64]{1,0:T(8,128)}, f32[3,3]{1,0:T(4,128)}) custom-call(f32[48,128]{1,0:T(8,128)} %ewald.1.packed_ref), custom_call_target="tpu_custom_call" | custom-call | tf_op jit(solution)/shard_map/unpack/pallas_call | solution.py:461

commit v4 on v3

--- a/solution.py
+++ b/solution.py
@@ -109,7 +109,7 @@
         return device((y_lo + p) % 2, z, (core + q) % 2, (v + j) % NV)
 
     far_first = [8, 7, 9, 6, 10, 5, 11, 4, 12, 3, 13, 2, 14, 1, 15]
-    plane = [(p, q, j) for p in (1, 0) for q in (1, 0) for j in (4, 6, 2, 5, 7, 3, 1, 0)]
+    plane = [(p, q, j) for p in (0, 1) for q in (1, 0) for j in (6, 2, 5, 7, 3, 4, 1, 0)]
     plane = [t for t in plane if t != (0, 0, 0)]
 
     def plane_slot(p, q, j):
@@ -150,8 +150,6 @@
     pos_s[3:6, :] = mid
     pos_s[6:9, :] = rest - mid
     pbuf[mine] = pos_s[...].astype(BF16)
-    for load in loads[1:]:
-        load.wait()
 
     y_to = 3 + 2 * core
     gathers = []
@@ -172,6 +170,8 @@
     signal(know.at[0], y_peer(1, core), y_peer(3, core))
     signal(know.at[3], z_peer(1), z_peer(15))
 
+    for load in loads[1:]:
+        load.wait()
     onehot = jnp.where(spec_ref[...].reshape(1, ATOMS) == iota((4, ATOMS), 0), 1.0, 0.0)
     lookup = dot(emb_ref[...], onehot, TN, PRECISE)
     hidden = (feat_ref[...].astype(F32) + lookup).astype(BF16)
@@ -180,6 +180,10 @@
     perm = select(c128 == ((r128 // 4) % 2) * 64 + (r128 % 4) * NZ + r128 // 8)
     gbuf[mine] = dot(perm, stacked).astype(BF16)
     gather_send(gbuf, g_ss, g_rs)
+    pl.semaphore_wait(know.at[3], 2)
+    signal(know.at[4], z_peer(2), z_peer(14))
+    pl.semaphore_wait(know.at[0], 2)
+    signal(know.at[1], x_peer(1), x_peer(3))
 
     mill = mil_ref[:, pl.ds(pl.multiple_of(mine * KL, KL), KL)].astype(F32)
     mrep[...] = jnp.zeros_like(mrep)
@@ -191,34 +195,30 @@
         tbuf[...] = dot(pbuf[slot], mrep_b, TN)
 
         def body(i, carry):
-            rows = pl.ds(pl.multiple_of(i * 32, 32), 32)
-            c, s = cos_sin_turns(tbuf[rows, :])
-            cbuf[slot, rows, :] = c.astype(BF16)
-            sbuf[slot, rows, :] = s.astype(BF16)
+            c, s = cos_sin_turns(tbuf[pl.ds(pl.multiple_of(i * 32, 32), 32), :])
+            rows = pl.ds(pl.multiple_of((slot % 2) * ATOMS + i * 32, 32), 32)
+            cbuf[slot // 2, rows, :] = c.astype(BF16)
+            sbuf[slot // 2, rows, :] = s.astype(BF16)
             return carry
 
         lax.fori_loop(0, ATOMS // 32, body, 0, unroll=2)
 
     def factors(slot):
         sp = gbuf[slot]
-        return dot(sp, cbuf[slot]), dot(sp, sbuf[slot])
+        rows = pl.ds(pl.multiple_of((slot % 2) * ATOMS, ATOMS), ATOMS)
+        return dot(sp, cbuf[slot // 2, rows, :]), dot(sp, sbuf[slot // 2, rows, :])
 
     phases(mine)
     others = ((0, y_lo * 2 + 1 - core), (1, (1 - y_lo) * 2), (2, (1 - y_lo) * 2 + 1))
     fc, fs = factors(mine)
-    pl.semaphore_wait(know.at[0], 2)
-    signal(know.at[1], x_peer(1), x_peer(3))
-    pl.semaphore_wait(know.at[3], 2)
-    signal(know.at[4], z_peer(2), z_peer(14))
     for k, slot in others:
         gather_wait(pbuf, p_ss, p_rs, slot, k)
         phases(slot)
         if k == 0:
+            pl.semaphore_wait(know.at[4], 2)
+            signal(know.at[5], z_peer(4), z_peer(12))
             pl.semaphore_wait(know.at[1], 2)
             signal(know.at[2], x_peer(1), x_peer(3))
-        if k == 1:
-            pl.semaphore_wait(know.at[4], 2)
-            signal(know.at[5], z_peer(4), z_peer(12))
     for k, slot in others:
         gather_wait(gbuf, g_ss, g_rs, slot, k)
         fck, fsk = factors(slot)
@@ -273,8 +273,9 @@
     pick_s = select((p == source) & (r_ < 8))
     for s in range(4):
         sp = gbuf[s]
-        tcbuf[s] = dot(sp, pick_c, TN).astype(BF16)
-        tsbuf[s] = dot(sp, pick_s, TN).astype(BF16)
+        rows = slice((s % 2) * ATOMS, (s % 2 + 1) * ATOMS)
+        tcbuf[s // 2, rows, :] = dot(sp, pick_c, TN).astype(BF16)
+        tsbuf[s // 2, rows, :] = dot(sp, pick_s, TN).astype(BF16)
 
     total = jnp.concatenate([facc[0, z], facc[1, z]], axis=0)
     for k in range(len(far_first) - 1, -1, -1):
@@ -317,6 +318,8 @@
             device_id=z_peer(i), device_id_type=MESH,
         ).wait_recv()
 
+    for cp in gathers + rs:
+        cp.wait_send()
     for i in far_first[::-1]:
         z_wait(ag_buf, ag_ss, ag_rs, i)
 
@@ -326,37 +329,35 @@
     xx = dot(select(pp == at + 4), terms).astype(BF16)
     yy = dot(select(pp == at + 12), terms).astype(BF16)
     wm = wm_s[...].astype(BF16)
-    lane = iota((8, 24, 128), 2)
-    lane8 = iota((8, 8, 128), 2)
+    lane = iota((2 * NV, 24, 128), 2)
+    lane8 = iota((2 * NV, 8, 128), 2)
     fins = []
-    for p, q in ((1, 1), (1, 0), (0, 1), (0, 0)):
-        slot = ((y_lo + p) % 2) * 2 + (core + q) % 2
-        alc[...] = dot(tcbuf[slot], terms)
-        als[...] = dot(tsbuf[slot], terms)
+    for p in (0, 1):
+        pair = (y_lo + p) % 2
+        alc[...] = dot(tcbuf[pair], terms)
+        als[...] = dot(tsbuf[pair], terms)
 
         def body(i, carry):
             rows = pl.ds(pl.multiple_of(i * 32, 32), 32)
             dbuf[rows, :] = (
-                cbuf[slot, rows, :].astype(F32) * alc[rows, :] - sbuf[slot, rows, :].astype(F32) * als[rows, :]
+                cbuf[pair, rows, :].astype(F32) * alc[rows, :] - sbuf[pair, rows, :].astype(F32) * als[rows, :]
             ).astype(BF16)
             return carry
 
-        lax.fori_loop(0, ATOMS // 32, body, 0, unroll=2)
-        out_a = (dot(cbuf[slot], xx, NT) + dot(sbuf[slot], yy, NT)).reshape(NV, PIECE, 128)
-        out_b = dot(dbuf[...], wm, NT).reshape(NV, PIECE, 128)
+        lax.fori_loop(0, 2 * ATOMS // 32, body, 0, unroll=4)
+        out_a = (dot(cbuf[pair], xx, NT) + dot(sbuf[pair], yy, NT)).reshape(2 * NV, PIECE, 128)
+        out_b = dot(dbuf[...], wm, NT).reshape(2 * NV, PIECE, 128)
         packed = jnp.where(lane < 64, out_a[:, 0:24, :], out_a[:, 24:48, :])
-        pushed = jnp.zeros((NV, 8, 128), F32)
+        pushed = jnp.zeros((2 * NV, 8, 128), F32)
         for g in range(6):
             pushed = jnp.where(lane8 // 16 == g, out_b[:, 8 * g : 8 * g + 8, :], pushed)
-        fin_snd[slot] = jnp.concatenate([packed, pushed], axis=1).astype(BF16)
+        fin_snd[pair] = jnp.concatenate([packed, pushed], axis=1).astype(BF16)
         for t in plane:
-            if t[:2] == (p, q):
+            if t[0] == p:
                 n = plane_slot(*t)
+                piece = ((core + t[1]) % 2) * NV + (v + t[2]) % NV
                 fins.append(
-                    send(
-                        fin_snd.at[slot, (v + t[2]) % NV], fin_buf.at[n], fin_ss.at[n], fin_rs.at[n],
-                        plane_peer(*t),
-                    )
+                    send(fin_snd.at[pair, piece], fin_buf.at[n], fin_ss.at[n], fin_rs.at[n], plane_peer(*t))
                 )
 
     for i in far_first[::-1]:
@@ -366,7 +367,9 @@
     for d in range(NZ):
         out_ref[32 + d : 33 + d, :] = zs_buf[d] * scales
 
-    acc = fin_snd[mine, v].astype(F32)
+    for cp in ag + pls + zs + fins:
+        cp.wait_send()
+    acc = fin_snd[y_lo, core * NV + v].astype(F32)
     for t, cp in zip(plane, fins):
         cp.wait_recv()
         acc = acc + fin_buf[plane_slot(*t)].astype(F32)
@@ -375,9 +378,6 @@
         unit = jnp.where(iota((8, 128), 1) % 16 == i, -TWO_PI / math.sqrt(K) / box_ref[i], unit)
     out_ref[0:24, :] = acc[0:24] * (1.0 / math.sqrt(K))
     out_ref[24:32, :] = acc[24:32] * unit
-
-    for cp in gathers + rs + ag + pls + zs + fins:
-        cp.wait_send()
 
 
 def unpack(packed_ref, feat_hbm, force_hbm, wgrad_hbm, vir_hbm, feat_s, force_s, wgrad_s, vir_s, sem):
@@ -415,10 +415,10 @@
         pltpu.VMEM((4, 16, ATOMS), BF16),
         pltpu.VMEM((4, 128, ATOMS), BF16),
         pltpu.VMEM((16, ATOMS), F32),
-        pltpu.VMEM((4, ATOMS, KL), BF16),
-        pltpu.VMEM((4, ATOMS, KL), BF16),
-        pltpu.VMEM((4, ATOMS, KL), BF16),
-        pltpu.VMEM((4, ATOMS, KL), BF16),
+        pltpu.VMEM((2, 2 * ATOMS, KL), BF16),
+        pltpu.VMEM((2, 2 * ATOMS, KL), BF16),
+        pltpu.VMEM((2, 2 * ATOMS, KL), BF16),
+        pltpu.VMEM((2, 2 * ATOMS, KL), BF16),
         pltpu.VMEM((ATOMS, KL), F32),
         pltpu.VMEM((16, KL), F32),
         pltpu.VMEM((128, KL), F32),
@@ -435,10 +435,10 @@
         pltpu.VMEM((32, 1, 128), F32),
         pltpu.VMEM((NZ, 1, 128), F32),
         pltpu.VMEM((8, KL), F32),
-        pltpu.VMEM((ATOMS, KL), F32),
-        pltpu.VMEM((ATOMS, KL), F32),
-        pltpu.VMEM((ATOMS, KL), BF16),
-        pltpu.VMEM((4, NV, 32, 128), BF16),
+        pltpu.VMEM((2 * ATOMS, KL), F32),
+        pltpu.VMEM((2 * ATOMS, KL), F32),
+        pltpu.VMEM((2 * ATOMS, KL), BF16),
+        pltpu.VMEM((2, 2 * NV, 32, 128), BF16),
         pltpu.VMEM((32, 32, 128), BF16),
         dma((8,)), dma((3,)), dma((3,)), dma((3,)), dma((3,)),
         dma((NZ,)), dma((NZ,)), dma((NZ,)), dma((NZ,)), dma((NZ,)), dma((NZ,)),

time: 49.8 us -> 49.7 us (level)
  no operation moved by 1% of the time
where the time goes in v4:
time: 49.7 us; the launch traced here: 49.5 us
  Pallas kernels  48.8 us (98%)
  between operations  0.64 us (1%)
    pallas_call x1, Pallas kernels, per_device(): pl.pallas_call(kernel, out_shape=jax.ShapeDtypeStruct((48, 128), F32), in...  47.3 us
    pallas_call x1, Pallas kernels, per_device(): pl.pallas_call(unpack, out_shape=results, in_specs=[vmem], out_specs=[any...  1.53 us

profile of v4, /device:TPU:1, one launch (start us, length us, event | category | flops | bytes accessed | tf_op | source)
XLA Modules:
  0.0 49.5 jit_solution(16937641496456279342)
XLA Ops:
  0.6 47.3 %ewald.1.packed_ref = f32[48,128]{1,0:T(8,128)} custom-call(bf16[64,384]{1,0:T(8,128)(2,1)} %feat_hbm.1, s32[384]{0:T(512)} %spec_hbm.1, f32[4,64]{1,0:T(4,128)} %emb_hbm.1, f32[3,384]{1,0:T(4,128)} %frac_hbm.1, f32[3]{0:T(128)} %box_hbm.1, s32[3,1024]{1,0:T(4,128)} %mil_hbm.1, f32[16,64]{1,0:T(8,128)} %w_hbm.1, bf16[64,384]{1,0:T(8,128)(2,1)} %cot_hbm.1), custom_call_target="tpu_custom_call" | custom-call | tf_op jit(solution)/shard_map/ewald/pallas_call | solution.py:448
  47.9 1.5 %unpack.1 = (f32[48,64]{1,0:T(8,128)}, f32[3,48]{1,0:T(4,128)}, f32[16,64]{1,0:T(8,128)}, f32[3,3]{1,0:T(4,128)}) custom-call(f32[48,128]{1,0:T(8,128)} %ewald.1.packed_ref), custom_call_target="tpu_custom_call" | custom-call | tf_op jit(solution)/shard_map/unpack/pallas_call | solution.py:461
